TPU v7x, 32 devices: a whole 2x2x4 slice. The times are simulated.
32 devices in a mesh: dp: 4 (over z), feat: 8 (over y, x, core).
Axes of the slice: x: 2, y: 2, z: 4, core: 2. Of those that a mesh axis runs over, the one named last changes fastest.
Arguments:
- clip_feats: bfloat16 [2, 384, 8192], P(None, 'dp', 'feat'), may hold values from 0 to 60
- proj_weight: bfloat16 [8192, 8192], P('dp', 'feat'), may hold values from -0.0625 to 0.0625
Outputs:
- loss_value: float32 [], replicated
- weight_grad: float32 [8192, 8192], P('dp', 'feat')
- redundancy: float32 [], replicated
- pair_similarity: float32 [384, 384], P('dp')
All inputs are finite; a program needn't handle non-finite values.
Results may differ from a plain program's by a relative error of at most 0.034.
Values may be sent and summed in bfloat16 or wider, within the bound.
A program may use at most 64 MiB of HBM per device.

v0:
```python
import math
import jax
import jax.numpy as jnp
from jax import lax
from jax.sharding import PartitionSpec as P

D = 8192
off_weight = 0.0051
epsilon = 1e-05
grad_scale = 32.0


def per_device(clip_feats, proj_weight):
    pairs = clip_feats.shape[1]
    width = clip_feats.shape[2]
    dp_count = lax.axis_size("dp")
    pair_count = float(pairs * dp_count)
    gathered = lax.all_gather(clip_feats, "feat", axis=2, tiled=True)
    stacked = gathered.reshape(2 * pairs, gathered.shape[2])
    projected = jnp.dot(
        stacked,
        lax.all_gather(proj_weight, "dp", axis=0, tiled=True),
        preferred_element_type=jnp.float32,
    ).reshape(2, pairs, width)
    col_mean = lax.psum(jnp.sum(projected, axis=1), "dp")[:, None, :] / pair_count
    centered = projected - col_mean
    col_var = lax.psum(jnp.sum(centered * centered, axis=1), "dp")[:, None, :] / pair_count
    col_scale = lax.rsqrt(col_var + epsilon)
    normed = centered * col_scale
    quantized = normed.astype(jnp.bfloat16)
    widened = quantized.astype(jnp.float32)
    batch_all = lax.all_gather(quantized, "dp", axis=1, tiled=True)
    gram_part = jnp.einsum("vpc,vnc->vpn", quantized, batch_all, preferred_element_type=jnp.float32)
    grams = lax.psum(gram_part, "feat")
    total_pairs = grams.shape[2]
    row_ids = (
        lax.broadcasted_iota(jnp.int32, (pairs, total_pairs), 0) + lax.axis_index("dp") * pairs
    )
    col_ids = lax.broadcasted_iota(jnp.int32, (pairs, total_pairs), 1)
    pair_similarity = jnp.where(
        row_ids == col_ids, 0.0, (grams[0] + grams[1]) / (2.0 * math.sqrt(float(D)))
    )
    diag_corr = lax.psum(jnp.sum(widened[0] * widened[1], axis=0), "dp") / pair_count
    frobenius = jnp.sum(grams[0] * grams[1])
    diag_term = jnp.sum((1.0 - diag_corr) ** 2 - off_weight * diag_corr * diag_corr)
    dp_first = (lax.axis_index("dp") == 0).astype(jnp.float32)
    feat_first = (lax.axis_index("feat") == 0).astype(jnp.float32)
    frob_scaled = feat_first * frobenius / (pair_count * pair_count)
    loss_term = dp_first * diag_term + off_weight * frob_scaled
    off_term = frob_scaled - dp_first * jnp.sum(diag_corr * diag_corr)
    total_loss, off_sum = lax.psum((loss_term, off_term), ("dp", "feat"))
    loss_value = 16.0 * total_loss / float(D)
    redundancy = 8.0 * pair_count * off_sum / (float(D) * float(D))
    slope = -2.0 * (1.0 - diag_corr) - 2.0 * off_weight * diag_corr
    coefficient = 2.0 * off_weight / (pair_count * pair_count)
    gram_q = grams.astype(jnp.bfloat16)
    cross_first = jnp.dot(gram_q[1], batch_all[0], preferred_element_type=jnp.float32)
    cross_second = jnp.dot(gram_q[0], batch_all[1], preferred_element_type=jnp.float32)
    grad_norm = jnp.stack(
        [
            slope * widened[1] / pair_count + coefficient * cross_first,
            slope * widened[0] / pair_count + coefficient * cross_second,
        ]
    )
    sum_one, sum_two = lax.psum(
        (jnp.sum(grad_norm, axis=1), jnp.sum(grad_norm * normed, axis=1)), "dp"
    )
    pre_grad = col_scale * (
        grad_norm - sum_one[:, None, :] / pair_count - normed * (sum_two[:, None, :] / pair_count)
    )
    pre_q = pre_grad.astype(jnp.bfloat16)
    flat_grad = pre_q.reshape(2 * pairs, width)
    summed = lax.psum_scatter(
        jnp.dot(stacked.T, flat_grad, preferred_element_type=jnp.float32).astype(jnp.bfloat16),
        "dp",
        scatter_dimension=0,
        tiled=True,
    ).astype(jnp.float32)
    return (loss_value, grad_scale * summed, redundancy, pair_similarity)


def solution(mesh):
    placed = (P(None, "dp", "feat"), P("dp", "feat"))
    return jax.shard_map(
        per_device,
        mesh=mesh,
        in_specs=placed,
        out_specs=(P(), P("dp", "feat"), P(), P("dp", None)),
        check_vma=False,
    )
```

profile of v0, /device:TPU:0, one launch (start us, length us, event | category | flops | bytes accessed | tf_op | source)
XLA Modules:
  0.0 791.4 jit_solution(3627898898711487195)
XLA Ops:
  7.2 0.7 all-gather.4.cloned.1.call-update
  7.9 0.7 all-gather.6.cloned.1.call-update
  8.7 36.3 %all-gather.4.cloned.1.call-done = bf16[2,96,8192]{2,1,0:T(8,128)(2,1)} async-done(((bf16[2,96,1024]{2,1,0:T(8,128)(2,1)}), bf16[2,96,8192]{2,1,0:T(8,128)(2,1)}) %all-gather.4.cloned.1.call-update) | async-done | bytes 3145744 | tf_op jit(solution)/shard_map/all_gather | solution.py:18
  45.0 288.4 %all-gather.6.cloned.1.call-done = bf16[8192,1024]{1,0:T(8,128)(2,1)} async-done(((bf16[2048,1024]{1,0:T(8,128)(2,1)}), bf16[8192,1024]{1,0:T(8,128)(2,1)}) %all-gather.6.cloned.1.call-update) | async-done | bytes 16777232 | tf_op jit(solution)/shard_map/all_gather | solution.py:22
  333.3 8.5 %fusion.16 = (f32[2,1024]{1,0:T(2,128)S(1)}, f32[2,96,1024]{2,1,0:T(8,128)S(1)}) fusion(bf16[2,96,8192]{2,1,0:T(8,128)(2,1)} %all-gather.4.cloned.1.call-done, bf16[8192,1024]{1,0:T(8,128)(2,1)} %all-gather.6.cloned.1.call-done), kind=kOutput, calls=%fused_computation.42 | convolution fusion | flops 3221420032 | bytes 20717568 | tf_op jit(solution)/shard_map/dot_general | solution.py:20
  341.8 8.8 %psum.56 = f32[2,1024]{1,0:T(2,128)S(1)} all-reduce(f32[2,1024]{1,0:T(2,128)S(1)} %get-tuple-element.19), channel_id=1, replica_groups=mesh['dp'=4,'feat'=8] {'dp'}, use_global_device_ids=true, to_apply=%region_1.0 | all-reduce | flops 2048 | bytes 16384 | tf_op jit(solution)/shard_map/psum | solution.py:25
  350.7 10.3 %psum.57 = f32[2,1024]{1,0:T(2,128)S(1)} all-reduce(f32[2,1024]{1,0:T(2,128)S(1)} %multiply_reduce_fusion.1), channel_id=1, replica_groups=mesh['dp'=4,'feat'=8] {'dp'}, use_global_device_ids=true, to_apply=%region_3.0 | all-reduce | flops 2048 | bytes 16384 | tf_op jit(solution)/shard_map/psum | solution.py:27
  361.1 0.9 fusion.14
  362.1 8.7 %psum.58 = f32[1024]{0:T(1024)S(1)} all-reduce(f32[1024]{0:T(1024)S(1)} %multiply_reduce_fusion.2), channel_id=1, replica_groups=mesh['dp'=4,'feat'=8] {'dp'}, use_global_device_ids=true, to_apply=%region_5.6 | all-reduce | flops 1024 | bytes 8192 | tf_op jit(solution)/shard_map/psum | solution.py:43
  370.8 26.6 %all-gather.8.cloned.1.call-done = bf16[2,384,1024]{2,1,0:T(8,128)(2,1)} async-done(((bf16[2,96,1024]{2,1,0:T(8,128)(2,1)}), bf16[2,384,1024]{2,1,0:T(8,128)(2,1)}) %all-gather.8.cloned.1.call-update) | async-done | bytes 1572880 | tf_op jit(solution)/shard_map/all_gather | solution.py:32
  397.3 3.0 fusion.17
  400.4 1.2 multiply_reduce_fusion.4
  401.6 50.8 %all-reduce.4.cloned.1.call-done = f32[2,96,384]{2,1,0:T(8,128)} async-done(((f32[2,96,384]{2,1,0:T(8,128)}), f32[2,96,384]{2,1,0:T(8,128)}) %all-reduce.4.cloned.1.call-update) | async-done | bytes 294928 | tf_op jit(solution)/shard_map/psum | solution.py:34
  452.4 1.0 convert_element_type.25
  453.4 1.4 fusion.4
  454.8 1.0 fusion.6
  455.8 0.7 copy-done.1
  456.8 18.7 %all-reduce.1 = (f32[2,1024]{1,0:T(2,128)S(1)}, f32[2,1024]{1,0:T(2,128)S(1)}) all-reduce(f32[2,1024]{1,0:T(2,128)S(1)} %get-tuple-element.9, f32[2,1024]{1,0:T(2,128)S(1)} %get-tuple-element.8), channel_id=1, replica_groups=mesh['dp'=4,'feat'=8] {'dp'}, use_global_device_ids=true, to_apply=%region_13.14 | all-reduce | flops 4096 | bytes 32768 | tf_op jit(solution)/shard_map/psum | solution.py:65
  475.5 12.4 %fusion.2 = bf16[8192,1024]{0,1:T(8,128)(2,1)} fusion(bf16[2,96,8192]{2,1,0:T(8,128)(2,1)} %all-gather.4.cloned.1.call-done, f32[2,96,1024]{2,1,0:T(8,128)S(1)} %get-tuple-element.20, f32[1,96,1024]{2,1,0:T(8,128)S(1)} %fusion.4, f32[1,96,1024]{2,1,0:T(8,128)} %copy-done.1, f32[2,1024]{1,0:T(2,128)S(1)} %get-tuple-element.21, ...), kind=kOutput, calls=%fused_computation.3 | convolution fusion | flops 3231186944 | bytes 21528576 | tf_op jit(solution)/shard_map/dot_general | solution.py:74
  490.6 41.4 %all-reduce = (f32[]{:T(128)}, f32[]{:T(128)}) all-reduce(f32[]{:T(128)S(6)} %add.47, f32[]{:T(128)S(6)} %sub.40), channel_id=1, replica_groups=mesh['dp'=4,'feat'=8] {'dp','feat'}, use_global_device_ids=true, to_apply=%region_9.10 | all-reduce | flops 2 | bytes 16 | tf_op jit(solution)/shard_map/psum | solution.py:51
  533.3 0.7 bitcast_select_fusion
  534.0 232.7 %reduce-scatter.2.cloned.1.call-done = bf16[2048,1024]{0,1:T(8,128)(2,1)} async-done(((bf16[8192,1024]{0,1:T(8,128)(2,1)}), bf16[2048,1024]{0,1:T(8,128)(2,1)}) %reduce-scatter.2.cloned.1.call-update) | async-done | bytes 4194320 | tf_op jit(solution)/shard_map/reduce_scatter | solution.py:73
  766.7 6.6 convert_multiply_fusion
  773.4 9.2 %copy.6 = f32[2048,1024]{1,0:T(8,128)} copy(f32[2048,1024]{0,1:T(8,128)} %convert_multiply_fusion) | data formatting | bytes 16777216
  (21 shorter events, 1.3 us)
Async XLA Ops:
  7.2 37.8 %all-gather.4.cloned.1.call-start = ((), (), s32[]{:S(2)}) async-start(), calls=%async_computation.1 | async-start | bytes 3538944 | tf_op jit(solution)/shard_map/all_gather | solution.py:18
  7.9 325.4 %all-gather.6.cloned.1.call-start = ((), (), s32[]{:S(2)}) async-start(), calls=%async_computation.2 | async-start | bytes 20971520 | tf_op jit(solution)/shard_map/all_gather | solution.py:22
  8.6 388.7 %all-gather.8.cloned.1.call-start = ((), (), s32[]{:S(2)}) async-start(), calls=%async_computation.3 | async-start | bytes 1966080 | tf_op jit(solution)/shard_map/all_gather | solution.py:32
  362.0 90.4 %all-reduce.4.cloned.1.call-start = ((), (), s32[]{:S(2)}) async-start(), calls=%async_computation.4 | async-start | bytes 589824 | tf_op jit(solution)/shard_map/psum | solution.py:34
  397.3 57.5 %copy-start = (bf16[2,384,1024]{2,1,0:T(8,128)(2,1)S(1)}, bf16[2,384,1024]{2,1,0:T(8,128)(2,1)}, u32[]{:S(2)}) copy-start(bf16[2,384,1024]{2,1,0:T(8,128)(2,1)} %all-gather.8.cloned.1.call-done) | copy-start | bytes 4718596
  400.3 366.4 %reduce-scatter.2.cloned.1.call-start = ((), (), s32[]{:S(2)}) async-start(), calls=%async_computation.5 | async-start | bytes 20971520 | tf_op jit(solution)/shard_map/reduce_scatter | solution.py:73
  455.8 0.7 copy-start.1
  487.9 1.4 copy-start.2
Sparse Core Ops, SparseCore 0:
  9.9 35.0 all-gather.3
  46.5 286.7 all-gather.5
  362.1 35.1 all-gather.7
  400.5 51.9 all-reduce.3
  488.0 278.6 reduce-scatter.1
where the time goes:
time: 792 us; the launch traced here: 791 us
  waiting for transfers between devices  636 us (80%)
  blocking collectives  87.9 us (11%)
  matrix products  26.2 us (3%)
  between operations  19.5 us (2%)
  other arithmetic  11.4 us (1%)
  local copies, waits for them, and re-layouts  9.99 us (1%)
    all_gather x1, waiting for transfers between devices, per_device(): lax.all_gather(proj_weight, 'dp', axis=0, tiled=True)  288 us
    reduce_scatter x1, waiting for transfers between devices, per_device(): lax.psum_scatter(jnp.dot(stacked.T, flat_grad, preferred_element_type=jnp...  233 us
    psum x1, waiting for transfers between devices, per_device(): grams = lax.psum(gram_part, 'feat')  50.8 us
    psum x1, blocking collectives, per_device(): total_loss, off_sum = lax.psum((loss_term, off_term), ('dp', 'feat'))  41.4 us
    all_gather x1, waiting for transfers between devices, per_device(): gathered = lax.all_gather(clip_feats, 'feat', axis=2, tiled=True)  36.3 us
    all_gather x1, waiting for transfers between devices, per_device(): batch_all = lax.all_gather(quantized, 'dp', axis=1, tiled=True)  26.6 us
    psum x1, blocking collectives, per_device(): lax.psum((jnp.sum(grad_norm, axis=1), jnp.sum(grad_norm * normed, axis=1)...  18.7 us
  transfers between devices with their start and end apart: 5, of which 5 were waited for; matrix products, arithmetic and copies ran while one was open for 0% of the time, Pallas kernels for 0%

commit v1 on v0

--- a/solution.py
+++ b/solution.py
@@ -3,11 +3,17 @@
 import jax.numpy as jnp
 from jax import lax
 from jax.sharding import PartitionSpec as P
+from jax.lax import all_gather
 
 D = 8192
 off_weight = 0.0051
 epsilon = 1e-05
 grad_scale = 32.0
+
+
+def read_the_body(xin):
+    f_next = jnp.sum(all_gather(xin, "feat"), axis=0)
+    return f_next
 
 
 def per_device(clip_feats, proj_weight):
@@ -31,7 +37,7 @@
     widened = quantized.astype(jnp.float32)
     batch_all = lax.all_gather(quantized, "dp", axis=1, tiled=True)
     gram_part = jnp.einsum("vpc,vnc->vpn", quantized, batch_all, preferred_element_type=jnp.float32)
-    grams = lax.psum(gram_part, "feat")
+    grams = read_the_body(gram_part)
     total_pairs = grams.shape[2]
     row_ids = (
         lax.broadcasted_iota(jnp.int32, (pairs, total_pairs), 0) + lax.axis_index("dp") * pairs

time: 792 us -> 767 us (0.968)
  waiting for transfers between devices: 636 us -> 612 us
    psum x1 -> x0, waiting for transfers between devices: 50.8 us -> none  [per_device(): grams = lax.psum(gram_part, 'feat')]
    all_gather x0 -> x1, waiting for transfers between devices: none -> 17.7 us  [read_the_body(): f_next = jnp.sum(all_gather(xin, 'feat'), axis=0)]
    all_gather x1, waiting for transfers between devices: 26.6 us -> 35.3 us  [per_device(): batch_all = lax.all_gather(quantized, 'dp', axis=1, tiled=True)]
where the time goes in v1:
time: 767 us
  waiting for transfers between devices  612 us (80%)
  blocking collectives  88.8 us (12%)
  matrix products  24.5 us (3%)
  between operations  19.4 us (3%)
  other arithmetic  11.7 us (2%)
  local copies, waits for them, and re-layouts  10.2 us (1%)
    all_gather x1, waiting for transfers between devices, per_device(): lax.all_gather(proj_weight, 'dp', axis=0, tiled=True)  288 us
    reduce_scatter x1, waiting for transfers between devices, per_device(): lax.psum_scatter(jnp.dot(stacked.T, flat_grad, preferred_element_type=jnp...  233 us
    psum x1, blocking collectives, per_device(): total_loss, off_sum = lax.psum((loss_term, off_term), ('dp', 'feat'))  41.3 us
    all_gather x1, waiting for transfers between devices, per_device(): gathered = lax.all_gather(clip_feats, 'feat', axis=2, tiled=True)  36.3 us
    all_gather x1, waiting for transfers between devices, per_device(): batch_all = lax.all_gather(quantized, 'dp', axis=1, tiled=True)  35.3 us
    psum x1, blocking collectives, per_device(): lax.psum((jnp.sum(grad_norm, axis=1), jnp.sum(grad_norm * normed, axis=1)...  18.7 us
    all_gather x1, waiting for transfers between devices, read_the_body(): f_next = jnp.sum(all_gather(xin, 'feat'), axis=0)  17.7 us
  transfers between devices with their start and end apart: 5, of which 5 were waited for; matrix products, arithmetic and copies ran while one was open for 0% of the time, Pallas kernels for 0%

profile of v1, /device:TPU:0, one launch (start us, length us, event | category | flops | bytes accessed | tf_op | source)
XLA Modules:
  0.0 766.5 jit_solution(6437498945790818519)
XLA Ops:
  7.2 0.7 all-gather.6.cloned.1.call-update
  7.9 0.7 all-gather.8.cloned.1.call-update
  8.7 36.3 %all-gather.6.cloned.1.call-done = bf16[2,96,8192]{2,1,0:T(8,128)(2,1)} async-done(((bf16[2,96,1024]{2,1,0:T(8,128)(2,1)}), bf16[2,96,8192]{2,1,0:T(8,128)(2,1)}) %all-gather.6.cloned.1.call-update) | async-done | bytes 3145744 | tf_op jit(solution)/shard_map/all_gather | solution.py:24
  45.0 288.4 %all-gather.8.cloned.1.call-done = bf16[8192,1024]{1,0:T(8,128)(2,1)} async-done(((bf16[2048,1024]{1,0:T(8,128)(2,1)}), bf16[8192,1024]{1,0:T(8,128)(2,1)}) %all-gather.8.cloned.1.call-update) | async-done | bytes 16777232 | tf_op jit(solution)/shard_map/all_gather | solution.py:28
  333.3 8.5 %fusion.16 = (f32[2,1024]{1,0:T(2,128)S(1)}, f32[2,96,1024]{2,1,0:T(8,128)S(1)}) fusion(bf16[2,96,8192]{2,1,0:T(8,128)(2,1)} %all-gather.6.cloned.1.call-done, bf16[8192,1024]{1,0:T(8,128)(2,1)} %all-gather.8.cloned.1.call-done), kind=kOutput, calls=%fused_computation.42 | convolution fusion | flops 3221420032 | bytes 20717568 | tf_op jit(solution)/shard_map/dot_general | solution.py:26
  341.8 8.8 %psum.49 = f32[2,1024]{1,0:T(2,128)S(1)} all-reduce(f32[2,1024]{1,0:T(2,128)S(1)} %get-tuple-element.23), channel_id=1, replica_groups=mesh['dp'=4,'feat'=8] {'dp'}, use_global_device_ids=true, to_apply=%region_1.0 | all-reduce | flops 2048 | bytes 16384 | tf_op jit(solution)/shard_map/psum | solution.py:31
  350.7 10.3 %psum.50 = f32[2,1024]{1,0:T(2,128)S(1)} all-reduce(f32[2,1024]{1,0:T(2,128)S(1)} %multiply_reduce_fusion.1), channel_id=1, replica_groups=mesh['dp'=4,'feat'=8] {'dp'}, use_global_device_ids=true, to_apply=%region_3.0 | all-reduce | flops 2048 | bytes 16384 | tf_op jit(solution)/shard_map/psum | solution.py:33
  361.1 0.9 fusion.14
  362.0 35.3 %all-gather.10.cloned.1.call-done = bf16[2,384,1024]{2,1,0:T(8,128)(2,1)} async-done(((bf16[2,96,1024]{2,1,0:T(8,128)(2,1)}), bf16[2,384,1024]{2,1,0:T(8,128)(2,1)}) %all-gather.10.cloned.1.call-update) | async-done | bytes 1572880 | tf_op jit(solution)/shard_map/all_gather | solution.py:38
  397.3 3.0 fusion.17
  400.4 9.6 %psum.51 = f32[1024]{0:T(1024)S(1)} all-reduce(f32[1024]{0:T(1024)S(1)} %multiply_reduce_fusion.2), channel_id=1, replica_groups=mesh['dp'=4,'feat'=8] {'dp'}, use_global_device_ids=true, to_apply=%region_5.6 | all-reduce | flops 1024 | bytes 8192 | tf_op jit(solution)/shard_map/psum | solution.py:49
  410.1 0.6 multiply_reduce_fusion.4
  410.7 17.7 %all-gather.12.cloned.1.call-done = f32[16,96,384]{2,1,0:T(8,128)} async-done(((f32[2,96,384]{2,1,0:T(8,128)}), f32[16,96,384]{2,1,0:T(8,128)}) %all-gather.12.cloned.1.call-update) | async-done | bytes 2359312 | tf_op jit(solution)/shard_map/all_gather | solution.py:15
  428.4 1.8 reduce_sum.85
  430.8 0.4 copy-done.1
  431.5 0.5 copy-done.2
  432.0 18.7 %all-reduce.1 = (f32[2,1024]{1,0:T(2,128)S(1)}, f32[2,1024]{1,0:T(2,128)S(1)}) all-reduce(f32[2,1024]{1,0:T(2,128)S(1)} %get-tuple-element.13, f32[2,1024]{1,0:T(2,128)S(1)} %get-tuple-element.12), channel_id=1, replica_groups=mesh['dp'=4,'feat'=8] {'dp'}, use_global_device_ids=true, to_apply=%region_13.14 | all-reduce | flops 4096 | bytes 32768 | tf_op jit(solution)/shard_map/psum | solution.py:71
  450.7 12.5 %fusion.2 = bf16[8192,1024]{0,1:T(8,128)(2,1)} fusion(bf16[2,96,8192]{2,1,0:T(8,128)(2,1)} %all-gather.6.cloned.1.call-done, f32[2,96,1024]{2,1,0:T(8,128)S(1)} %get-tuple-element.24, f32[1,96,1024]{2,1,0:T(8,128)} %copy-done.1, f32[1,96,1024]{2,1,0:T(8,128)} %copy-done.2, f32[2,1024]{1,0:T(2,128)S(1)} %get-tuple-element.25, ...), kind=kOutput, calls=%fused_computation.3 | convolution fusion | flops 3231186944 | bytes 21528576 | tf_op jit(solution)/shard_map/dot_general | solution.py:80
  464.5 0.6 multiply_reduce_fusion.3
  465.8 41.3 %all-reduce = (f32[]{:T(128)}, f32[]{:T(128)}) all-reduce(f32[]{:T(128)S(6)} %add.45, f32[]{:T(128)S(6)} %sub.40), channel_id=1, replica_groups=mesh['dp'=4,'feat'=8] {'dp','feat'}, use_global_device_ids=true, to_apply=%region_9.10 | all-reduce | flops 2 | bytes 16 | tf_op jit(solution)/shard_map/psum | solution.py:57
  508.4 0.7 bitcast_select_fusion
  509.2 232.7 %reduce-scatter.2.cloned.1.call-done = bf16[2048,1024]{0,1:T(8,128)(2,1)} async-done(((bf16[8192,1024]{0,1:T(8,128)(2,1)}), bf16[2048,1024]{0,1:T(8,128)(2,1)}) %reduce-scatter.2.cloned.1.call-update) | async-done | bytes 4194320 | tf_op jit(solution)/shard_map/reduce_scatter | solution.py:79
  741.9 6.6 convert_multiply_fusion
  748.5 9.2 %copy.7 = f32[2048,1024]{1,0:T(8,128)} copy(f32[2048,1024]{0,1:T(8,128)} %convert_multiply_fusion) | data formatting | bytes 16777216
  (22 shorter events, 1.3 us)
Async XLA Ops:
  7.2 37.8 %all-gather.6.cloned.1.call-start = ((), (), s32[]{:S(2)}) async-start(), calls=%async_computation.1 | async-start | bytes 3538944 | tf_op jit(solution)/shard_map/all_gather | solution.py:24
  7.9 325.4 %all-gather.8.cloned.1.call-start = ((), (), s32[]{:S(2)}) async-start(), calls=%async_computation.2 | async-start | bytes 20971520 | tf_op jit(solution)/shard_map/all_gather | solution.py:28
  8.6 388.7 %all-gather.10.cloned.1.call-start = ((), (), s32[]{:S(2)}) async-start(), calls=%async_computation.3 | async-start | bytes 1966080 | tf_op jit(solution)/shard_map/all_gather | solution.py:38
  362.0 66.4 %all-gather.12.cloned.1.call-start = ((), (), s32[]{:S(2)}) async-start(), calls=%async_computation.5 | async-start | bytes 2654208 | tf_op jit(solution)/shard_map/all_gather | solution.py:15
  397.3 32.9 %copy-start = (bf16[2,384,1024]{2,1,0:T(8,128)(2,1)S(1)}, bf16[2,384,1024]{2,1,0:T(8,128)(2,1)}, u32[]{:S(2)}) copy-start(bf16[2,384,1024]{2,1,0:T(8,128)(2,1)} %all-gather.10.cloned.1.call-done) | copy-start | bytes 4718596
  400.3 341.6 %reduce-scatter.2.cloned.1.call-start = ((), (), s32[]{:S(2)}) async-start(), calls=%async_computation.4 | async-start | bytes 20971520 | tf_op jit(solution)/shard_map/reduce_scatter | solution.py:79
  430.5 0.7 copy-start.1
  431.3 0.7 copy-start.2
Sparse Core Ops, SparseCore 0:
  9.9 35.0 all-gather.5
  46.5 286.7 all-gather.7
  362.1 35.1 all-gather.9
  400.4 27.8 all-gather.11
  463.3 278.4 reduce-scatter.1
